TPU v7x, 32 devices: a whole 2x2x4 slice. The times are simulated.
32 devices in a mesh: ctx: 8 (over z, y), fsdp: 4 (over x, core).
Axes of the slice: x: 2, y: 2, z: 4, core: 2. Of those that a mesh axis runs over, the one named last changes fastest.
Arguments:
- tokens: bfloat16 [3, 4, 2048, 1024], P(None, 'fsdp', 'ctx'), may hold values from -6 to 6
- w_router: float32 [1024], replicated, may hold values from -0.1875 to 0.1875
- gain_attn: float32 [1024], replicated, may hold values from 0.1 to 1.9
- w_qkv: bfloat16 [1024, 3072], P('fsdp'), may hold values from -0.1875 to 0.1875
- w_out: bfloat16 [1024, 1024], P('fsdp'), may hold values from -1 to 1
- gain_mlp: float32 [1024], replicated, may hold values from 0.1 to 1.9
- w_up: bfloat16 [1024, 4096], P('fsdp'), may hold values from -0.1875 to 0.1875
- w_down: bfloat16 [4096, 1024], P('fsdp'), may hold values from -0.09375 to 0.09375
- routed: int32 [3, 4, 256], P(None, 'fsdp', 'ctx'), may hold values from 0 to 2047, as said below
- deal: int32 [16], replicated, may hold values from 0 to 15, as said below
- cotangent: bfloat16 [3, 4, 2048, 1024], P(None, 'fsdp', 'ctx'), may hold values from -6 to 6
Outputs:
- output: bfloat16 [3, 4, 2048, 1024], P(None, 'fsdp', 'ctx')
- input_grad: bfloat16 [3, 4, 2048, 1024], P(None, 'fsdp', 'ctx')
- grad_router: float32 [1024], P(('ctx', 'fsdp'))
- grad_gain_attn: float32 [1024], P(('ctx', 'fsdp'))
- grad_qkv: float32 [1024, 3072], P(('ctx', 'fsdp'))
- grad_out: float32 [1024, 1024], P(('ctx', 'fsdp'))
- grad_gain_mlp: float32 [1024], P(('ctx', 'fsdp'))
- grad_up: float32 [1024, 4096], P(('ctx', 'fsdp'))
- grad_down: float32 [4096, 1024], P(('ctx', 'fsdp'))
Inputs may be any that keep to these rules, and one draw needn't show every extreme that they name: `routed`: for each micro-batch and sequence the indices rise; entries j * 32 to (j + 1) * 32 - 1 are distinct stored rows among j * 256 to (j + 1) * 256 - 1, and include j * 256 and (j + 1) * 256 - 1. `deal`: each initial span appears once; stored spans 2 j and 2 j + 1 hold initial spans c and 15 - c.
All inputs are finite; a program needn't handle non-finite values.
Results may differ from a plain program's by a relative error of at most 0.012.
Values may be sent and summed in bfloat16 or wider, within the bound.
No kernel may reach another device: no remote copies, remote signals or barrier semaphores. Data moves between devices by JAX's collectives and lax.ppermute only.
A program may use at most 256 MiB of HBM per device.

v0:
```python
import jax
import jax.numpy as jnp
from jax import lax
from jax.sharding import PartitionSpec as P

HEADS = 16
HEAD_DIM = 64
BLOCK = 256
EPSILON = 1e-06
MASKED = -1e30
HIGHEST = lax.Precision.HIGHEST


def rms_norm(values, gain):
    factor = lax.rsqrt(jnp.mean(values * values, axis=-1, keepdims=True) + EPSILON)
    return values * factor * gain


def exact_gelu(values):
    return jax.nn.gelu(values, approximate=False)


def fetch(w_qkv, w_out, w_up, w_down):
    return (
        lax.all_gather(w_qkv, "fsdp", axis=0, tiled=True),
        lax.all_gather(w_out, "fsdp", axis=0, tiled=True),
        lax.all_gather(w_up, "fsdp", axis=0, tiled=True),
        lax.all_gather(w_down, "fsdp", axis=0, tiled=True),
    )


def lookup(table, index):
    hits = index[..., None] == jnp.arange(table.shape[0], dtype=jnp.int32)
    return jnp.sum(jnp.where(hits, table, 0), axis=-1)


def outer_sum(left, right):
    return lax.dot_general(
        left, right, (((0,), (0,)), ((), ())), preferred_element_type=jnp.float32
    )


def gather_rows(pieces, column):
    return jnp.concatenate([piece[column] for piece in pieces], axis=0)


def shards(
    tokens, w_router, gain_attn, w_qkv, w_out, gain_mlp, w_up, w_down, routed, deal, cotangent
):
    micros, tok_dev, width = (tokens.shape[0], tokens.shape[2], tokens.shape[3])
    span = tok_dev // 2
    rank = lax.axis_index("ctx")
    storage = routed[:, 0, :]
    local_rows = storage - rank * tok_dev
    anchor = lookup(deal, storage // span) * span + storage % span
    own_blocks = anchor // BLOCK
    all_blocks = lax.all_gather(own_blocks, "ctx", axis=1, tiled=True)
    factor = HEAD_DIM ** (-0.5)
    outputs, in_grads, kept = ([], [], [])
    sum_router = jnp.zeros((width,), jnp.float32)
    sum_gain_attn = jnp.zeros((width,), jnp.float32)
    sum_gain_mlp = jnp.zeros((width,), jnp.float32)
    for micro in range(micros):
        full_qkv, full_out, full_up, full_down = fetch(w_qkv, w_out, w_up, w_down)
        resid = tokens[micro, 0].astype(jnp.float32)
        grad_in = cotangent[micro, 0].astype(jnp.float32)
        rows_index = local_rows[micro]
        rows = jnp.take(resid, rows_index, axis=0)
        count = rows.shape[0]
        gate = jax.nn.sigmoid(jnp.dot(rows, w_router, precision=HIGHEST))
        norm1, norm1_back = jax.vjp(rms_norm, rows, gain_attn)
        norm1_low = norm1.astype(jnp.bfloat16)
        qkv = jnp.dot(norm1_low, full_qkv, preferred_element_type=jnp.float32).astype(jnp.bfloat16)
        queries = qkv[:, :width]
        keys_local = qkv[:, width : 2 * width]
        values_local = qkv[:, 2 * width :]
        keys_all, values_all = (
            lax.all_gather(keys_local, "ctx", axis=0, tiled=True),
            lax.all_gather(values_local, "ctx", axis=0, tiled=True),
        )
        total = keys_all.shape[0]
        query_heads = queries.reshape(count, HEADS, HEAD_DIM)
        key_heads = keys_all.reshape(total, HEADS, HEAD_DIM)
        value_heads = values_all.reshape(total, HEADS, HEAD_DIM)
        visible = all_blocks[micro][None, :] <= own_blocks[micro][:, None]
        scores = (
            jnp.einsum("qhd,khd->hqk", query_heads, key_heads, preferred_element_type=jnp.float32)
            * factor
        )
        scores = jnp.where(visible[None], scores, MASKED)
        probs = jax.nn.softmax(scores, axis=-1)
        probs_low = probs.astype(jnp.bfloat16)
        attended = jnp.einsum(
            "hqk,khd->qhd", probs_low, value_heads, preferred_element_type=jnp.float32
        )
        attended_low = attended.reshape(count, width).astype(jnp.bfloat16)
        attn = jnp.dot(attended_low, full_out, preferred_element_type=jnp.float32)
        mid = rows + attn
        norm2, norm2_back = jax.vjp(rms_norm, mid, gain_mlp)
        norm2_low = norm2.astype(jnp.bfloat16)
        hidden = jnp.dot(norm2_low, full_up, preferred_element_type=jnp.float32)
        act, gelu_back = jax.vjp(exact_gelu, hidden)
        act_low = act.astype(jnp.bfloat16)
        mlp = jnp.dot(act_low, full_down, preferred_element_type=jnp.float32)
        branch = attn + mlp
        outputs.append(resid.at[rows_index].set(rows + gate[:, None] * branch).astype(jnp.bfloat16))
        cot_rows = jnp.take(grad_in, rows_index, axis=0)
        d_branch = gate[:, None] * cot_rows
        d_mlp = d_branch.astype(jnp.bfloat16)
        d_logit = jnp.sum(cot_rows * branch, axis=-1) * gate * (1.0 - gate)
        d_act = jnp.dot(d_mlp, full_down.T, preferred_element_type=jnp.float32)
        d_hidden = gelu_back(d_act)[0].astype(jnp.bfloat16)
        d_norm2 = jnp.dot(d_hidden, full_up.T, preferred_element_type=jnp.float32)
        d_mid, d_gain2 = norm2_back(d_norm2)
        d_attn = (d_branch + d_mid).astype(jnp.bfloat16)
        d_attended = jnp.dot(d_attn, full_out.T, preferred_element_type=jnp.float32).astype(
            jnp.bfloat16
        )
        d_heads = d_attended.reshape(count, HEADS, HEAD_DIM)
        d_probs = jnp.einsum(
            "qhd,khd->hqk", d_heads, value_heads, preferred_element_type=jnp.float32
        )
        weighted = jnp.sum(probs * d_probs, axis=-1, keepdims=True)
        d_scores = (probs * (d_probs - weighted)).astype(jnp.bfloat16)
        d_query = (
            jnp.einsum("hqk,khd->qhd", d_scores, key_heads, preferred_element_type=jnp.float32)
            * factor
        )
        d_key_part = (
            jnp.einsum("hqk,qhd->khd", d_scores, query_heads, preferred_element_type=jnp.float32)
            * factor
        )
        d_value_part = jnp.einsum(
            "hqk,qhd->khd", probs_low, d_heads, preferred_element_type=jnp.float32
        )
        d_keys, d_values = (
            lax.psum_scatter(
                d_key_part.reshape(total, width), "ctx", scatter_dimension=0, tiled=True
            ),
            lax.psum_scatter(
                d_value_part.reshape(total, width), "ctx", scatter_dimension=0, tiled=True
            ),
        )
        d_qkv = jnp.concatenate([d_query.reshape(count, width), d_keys, d_values], axis=1).astype(
            jnp.bfloat16
        )
        d_norm1 = jnp.dot(d_qkv, full_qkv.T, preferred_element_type=jnp.float32)
        d_rows_norm, d_gain1 = norm1_back(d_norm1)
        d_rows = cot_rows + d_mid + d_rows_norm + d_logit[:, None] * w_router
        in_grads.append(grad_in.at[rows_index].set(d_rows).astype(jnp.bfloat16))
        sum_router = sum_router + jnp.dot(d_logit, rows, precision=HIGHEST)
        sum_gain_attn = sum_gain_attn + d_gain1
        sum_gain_mlp = sum_gain_mlp + d_gain2
        kept.append((norm1_low, d_qkv, attended_low, d_attn, norm2_low, d_hidden, act_low, d_mlp))
    stacked_rows = tuple((gather_rows(kept, column) for column in range(8)))
    grad_qkv = outer_sum(stacked_rows[0], stacked_rows[1])
    grad_out = outer_sum(stacked_rows[2], stacked_rows[3])
    grad_up = outer_sum(stacked_rows[4], stacked_rows[5])
    grad_down = outer_sum(stacked_rows[6], stacked_rows[7])
    summed = (
        lax.psum_scatter(sum_router, ("ctx", "fsdp"), scatter_dimension=0, tiled=True),
        lax.psum_scatter(sum_gain_attn, ("ctx", "fsdp"), scatter_dimension=0, tiled=True),
        lax.psum_scatter(grad_qkv, ("ctx", "fsdp"), scatter_dimension=0, tiled=True),
        lax.psum_scatter(grad_out, ("ctx", "fsdp"), scatter_dimension=0, tiled=True),
        lax.psum_scatter(sum_gain_mlp, ("ctx", "fsdp"), scatter_dimension=0, tiled=True),
        lax.psum_scatter(grad_up, ("ctx", "fsdp"), scatter_dimension=0, tiled=True),
        lax.psum_scatter(grad_down, ("ctx", "fsdp"), scatter_dimension=0, tiled=True),
    )
    output = jnp.stack(outputs)[:, None]
    input_grad = jnp.stack(in_grads)[:, None]
    return (
        output,
        input_grad,
        summed[0],
        summed[1],
        summed[2],
        summed[3],
        summed[4],
        summed[5],
        summed[6],
    )


def solution(mesh):
    placed = (
        P(None, "fsdp", "ctx", None),
        P(),
        P(),
        P("fsdp", None),
        P("fsdp", None),
        P(),
        P("fsdp", None),
        P("fsdp", None),
        P(None, "fsdp", "ctx"),
        P(),
        P(None, "fsdp", "ctx", None),
    )
    return jax.shard_map(
        shards,
        mesh=mesh,
        in_specs=placed,
        out_specs=(
            P(None, "fsdp", "ctx", None),
            P(None, "fsdp", "ctx", None),
            P(("ctx", "fsdp")),
            P(("ctx", "fsdp")),
            P(("ctx", "fsdp"), None),
            P(("ctx", "fsdp"), None),
            P(("ctx", "fsdp")),
            P(("ctx", "fsdp"), None),
            P(("ctx", "fsdp"), None),
        ),
        check_vma=False,
    )
```

profile of v0, /device:TPU:14, one launch (start us, length us, event | category | flops | bytes accessed | tf_op | source)
XLA Modules:
  0.0 1517.1 jit_solution(7598239076845456931)
XLA Ops:
  10.8 25.0 %all-gather = s32[8,32,3]{1,2,0:T(4,128)S(1)} all-gather(s32[1,32,3]{1,2,0:T(4,128)S(1)} %bitcast.289), channel_id=1, replica_groups=mesh['ctx'=8,'fsdp'=4] {'ctx'}, dimensions={0}, use_global_device_ids=true | all-gather | bytes 3456 | tf_op jit(solution)/shard_map/all_gather | solution.py:57
  40.3 2.7 bitcast_convert_fusion.2
  46.3 9.9 all-gather.6.cloned.1.call-done
  56.2 4.0 convolution_convert_fusion.2
  60.4 29.6 %all_gather.44 = bf16[256,1024]{1,0:T(8,128)(2,1)S(1)} all-gather(bf16[32,1024]{1,0:T(8,128)(2,1)S(1)} %get-tuple-element.89), channel_id=1, replica_groups=mesh['ctx'=8,'fsdp'=4] {'ctx'}, dimensions={0}, use_global_device_ids=true | all-gather | bytes 589824 | tf_op jit(solution)/shard_map/all_gather | solution.py:78
  90.2 31.1 %all_gather.42 = bf16[256,1024]{1,0:T(8,128)(2,1)S(1)} all-gather(bf16[32,1024]{1,0:T(8,128)(2,1)S(1)} %get-tuple-element.90), channel_id=1, replica_groups=mesh['ctx'=8,'fsdp'=4] {'ctx'}, dimensions={0}, use_global_device_ids=true | all-gather | bytes 589824 | tf_op jit(solution)/shard_map/all_gather | solution.py:79
  124.5 2.8 multiply_reduce_fusion.22
  127.5 12.7 all-gather.10.cloned.1.call-done
  140.3 4.9 fusion.285
  145.2 54.8 %all-gather.12.cloned.1.call-done = bf16[4096,1024]{1,0:T(8,128)(2,1)} async-done(((bf16[1024,1024]{1,0:T(8,128)(2,1)}), bf16[4096,1024]{1,0:T(8,128)(2,1)}) %all-gather.12.cloned.1.call-update) | async-done | bytes 8388624 | tf_op jit(solution)/shard_map/all_gather | solution.py:28
  200.0 7.5 add_convert_fusion.2
  207.6 3.2 multiply_reduce_fusion.5
  213.0 3.4 fusion.164
  249.8 5.6 convolution_add_fusion.2
  255.4 27.9 %reduce-scatter.13.cloned.1.call-done = f32[32,1024]{1,0:T(8,128)} async-done(((f32[256,1024]{1,0:T(8,128)}), f32[32,1024]{1,0:T(8,128)}) %reduce-scatter.13.cloned.1.call-update) | async-done | bytes 131088 | tf_op jit(solution)/shard_map/reduce_scatter | solution.py:140
  284.9 64.6 %reduce-scatter.11.cloned.1.call-done = f32[32,1024]{1,0:T(8,128)} async-done(((f32[256,1024]{1,0:T(8,128)}), f32[32,1024]{1,0:T(8,128)}) %reduce-scatter.11.cloned.1.call-update) | async-done | bytes 131088 | tf_op jit(solution)/shard_map/reduce_scatter | solution.py:137
  350.4 6.3 multiply_reduce_fusion.8
  356.7 4.0 convolution_convert_fusion.1
  363.0 4.0 convolution_convert_fusion
  369.3 29.4 %all_gather.51 = bf16[256,1024]{1,0:T(8,128)(2,1)} all-gather(bf16[32,1024]{1,0:T(8,128)(2,1)} %get-tuple-element.95), channel_id=1, replica_groups=mesh['ctx'=8,'fsdp'=4] {'ctx'}, dimensions={0}, use_global_device_ids=true | all-gather | bytes 589824 | tf_op jit(solution)/shard_map/all_gather | solution.py:78
  400.7 34.1 %all_gather.50 = bf16[256,1024]{1,0:T(8,128)(2,1)} all-gather(bf16[32,1024]{1,0:T(8,128)(2,1)} %get-tuple-element.96), channel_id=1, replica_groups=mesh['ctx'=8,'fsdp'=4] {'ctx'}, dimensions={0}, use_global_device_ids=true | all-gather | bytes 589824 | tf_op jit(solution)/shard_map/all_gather | solution.py:79
  436.8 33.5 %all_gather.49 = bf16[256,1024]{1,0:T(8,128)(2,1)} all-gather(bf16[32,1024]{1,0:T(8,128)(2,1)} %get-tuple-element.92), channel_id=1, replica_groups=mesh['ctx'=8,'fsdp'=4] {'ctx'}, dimensions={0}, use_global_device_ids=true | all-gather | bytes 589824 | tf_op jit(solution)/shard_map/all_gather | solution.py:78
  472.4 33.4 %all_gather.48 = bf16[256,1024]{1,0:T(8,128)(2,1)} all-gather(bf16[32,1024]{1,0:T(8,128)(2,1)} %get-tuple-element.93), channel_id=1, replica_groups=mesh['ctx'=8,'fsdp'=4] {'ctx'}, dimensions={0}, use_global_device_ids=true | all-gather | bytes 589824 | tf_op jit(solution)/shard_map/all_gather | solution.py:79
  511.4 3.0 fusion.16
  524.0 3.0 fusion.17
  533.5 5.1 fusion.286
  538.6 7.6 add_convert_fusion.1
  546.3 3.2 multiply_reduce_fusion.4
  551.7 4.2 add_convert_fusion
  556.0 3.2 multiply_reduce_fusion.3
  563.7 3.3 fusion.158
  573.0 3.3 fusion.152
  586.9 3.8 fusion.104
  591.8 44.8 %reduce-scatter.17.cloned.1.call-done = f32[32,1024]{1,0:T(8,128)} async-done(((f32[256,1024]{1,0:T(8,128)}), f32[32,1024]{1,0:T(8,128)}) %reduce-scatter.17.cloned.1.call-update) | async-done | bytes 131088 | tf_op jit(solution)/shard_map/reduce_scatter | solution.py:140
  637.5 65.4 %reduce-scatter.21.cloned.1.call-done = f32[32,1024]{1,0:T(8,128)} async-done(((f32[256,1024]{1,0:T(8,128)}), f32[32,1024]{1,0:T(8,128)}) %reduce-scatter.21.cloned.1.call-update) | async-done | bytes 131088 | tf_op jit(solution)/shard_map/reduce_scatter | solution.py:140
  703.8 65.0 %reduce-scatter.15.cloned.1.call-done = f32[32,1024]{1,0:T(8,128)} async-done(((f32[256,1024]{1,0:T(8,128)}), f32[32,1024]{1,0:T(8,128)}) %reduce-scatter.15.cloned.1.call-update) | async-done | bytes 131088 | tf_op jit(solution)/shard_map/reduce_scatter | solution.py:137
  769.8 65.2 %reduce-scatter.19.cloned.1.call-done = f32[32,1024]{1,0:T(8,128)} async-done(((f32[256,1024]{1,0:T(8,128)}), f32[32,1024]{1,0:T(8,128)}) %reduce-scatter.19.cloned.1.call-update) | async-done | bytes 131088 | tf_op jit(solution)/shard_map/reduce_scatter | solution.py:137
  835.9 6.4 fusion.45
  845.7 8.2 fusion.39
  855.0 8.1 fusion.33
  866.5 5.1 convolution_add_fusion.1
  873.8 5.8 convolution_add_fusion
  891.7 4.9 fusion.93
  896.8 3.3 multiply_reduce_fusion.7
  905.1 39.6 %all-reduce.3 = (f32[1024]{0:T(1024)S(1)}, f32[1024]{0:T(1024)S(1)}, f32[1024]{0:T(1024)S(1)}) all-reduce(f32[1024]{0:T(1024)S(1)} %add_add_fusion.11, f32[1024]{0:T(1024)S(1)} %add_add_fusion.10, f32[1024]{0:T(1024)} %add_add_fusion.9), channel_id=8, replica_groups=mesh['ctx'=8,'fsdp'=4] {'ctx','fsdp'}, use_global_device_ids=true, to_apply=%region_37.39.clone | all-reduce | flops 3072 | bytes 24576
  950.4 185.2 %reduce-scatter.23.cloned.1.call-done = f32[32,3072]{1,0:T(8,128)} async-done(((f32[1024,3072]{1,0:T(8,128)}), f32[32,3072]{1,0:T(8,128)}) %reduce-scatter.23.cloned.1.call-update) | async-done | bytes 393232 | tf_op jit(solution)/shard_map/reduce_scatter | solution.py:163
  1135.5 187.4 %reduce-scatter.29.cloned.1.call-done = f32[128,1024]{1,0:T(8,128)} async-done(((f32[4096,1024]{1,0:T(8,128)}), f32[128,1024]{1,0:T(8,128)}) %reduce-scatter.29.cloned.1.call-update) | async-done | bytes 524304 | tf_op jit(solution)/shard_map/reduce_scatter | solution.py:167
  1323.0 187.3 %reduce-scatter.27.cloned.1.call-done = f32[32,4096]{1,0:T(8,128)} async-done(((f32[1024,4096]{1,0:T(8,128)}), f32[32,4096]{1,0:T(8,128)}) %reduce-scatter.27.cloned.1.call-update) | async-done | bytes 524304 | tf_op jit(solution)/shard_map/reduce_scatter | solution.py:166
  (474 shorter events, 145.3 us)
Async XLA Ops:
  7.2 29.8 %copy-start.37 = (bf16[3,1,256,1024]{3,2,1,0:T(8,128)(2,1)S(1)}, bf16[3,1,256,1024]{3,2,1,0:T(8,128)(2,1)}, u32[]{:S(2)}) copy-start(bf16[3,1,256,1024]{3,2,1,0:T(8,128)(2,1)} %param.13) | copy-start | bytes 4718596
  7.2 49.0 %all-gather.6.cloned.1.call-start = ((), (), s32[]{:S(2)}) async-start(), calls=%async_computation.10 | async-start | bytes 7864320 | tf_op jit(solution)/shard_map/all_gather | solution.py:25
  7.9 116.5 %all-gather.8.cloned.1.call-start = ((), (), s32[]{:S(2)}) async-start(), calls=%async_computation.11 | async-start | bytes 2621440 | tf_op jit(solution)/shard_map/all_gather | solution.py:26
  8.7 131.6 %all-gather.10.cloned.1.call-start = ((), (), s32[]{:S(2)}) async-start(), calls=%async_computation.12 | async-start | bytes 10485760 | tf_op jit(solution)/shard_map/all_gather | solution.py:27
  9.4 190.6 %all-gather.12.cloned.1.call-start = ((), (), s32[]{:S(2)}) async-start(), calls=%async_computation.13 | async-start | bytes 10485760 | tf_op jit(solution)/shard_map/all_gather | solution.py:28
  10.0 273.3 %reduce-scatter.13.cloned.1.call-start = ((), (), s32[]{:S(2)}) async-start(), calls=%async_computation.15 | async-start | bytes 1179648 | tf_op jit(solution)/shard_map/reduce_scatter | solution.py:140
  10.2 26.8 %copy-start.112 = (s32[3,32]{1,0:T(4,128)}, s32[3,32]{1,0:T(4,128)S(1)}, u32[]{:S(2)}) copy-start(s32[3,32]{1,0:T(4,128)S(1)} %get-tuple-element.119) | copy-start | bytes 1156
  43.1 17.1 %copy-start.3 = (f32[256,1024]{1,0:T(8,128)}, f32[256,1024]{1,0:T(8,128)S(1)}, u32[]{:S(2)}) copy-start(f32[256,1024]{1,0:T(8,128)S(1)} %get-tuple-element.82) | copy-start | bytes 3145732
  43.8 167.0 %copy-start.22 = (f32[32,1024]{1,0:T(8,128)}, f32[32,1024]{1,0:T(8,128)S(1)}, u32[]{:S(2)}) copy-start(f32[32,1024]{1,0:T(8,128)S(1)} %gather_fusion.3) | copy-start | bytes 393220
  44.6 15.6 %copy-start.128 = (f32[32]{0:T(128)}, f32[32]{0:T(128)S(1)}, u32[]{:S(2)}) copy-start(f32[32]{0:T(128)S(1)} %fusion.256) | copy-start | bytes 388
  46.2 78.3 %copy-start.123 = (f32[32]{0:T(128)}, f32[32]{0:T(128)S(1)}, u32[]{:S(2)}) copy-start(f32[32]{0:T(128)S(1)} %fusion.32) | copy-start | bytes 388
  46.3 13.9 copy-start.64
  60.4 63.9 %copy-start.47 = (bf16[32,16,64]{2,1,0:T(8,128)(2,1)}, bf16[32,16,64]{2,1,0:T(8,128)(2,1)S(1)}, u32[]{:S(2)}) copy-start(bf16[32,16,64]{2,1,0:T(8,128)(2,1)S(1)} %reshape.442) | copy-start | bytes 196612
  90.0 34.5 %copy-start.102 = (pred[32]{0:T(512)(128)(4,1)S(1)}, pred[32]{0:T(512)(128)(4,1)}, u32[]{:S(2)}) copy-start(pred[32]{0:T(512)(128)(4,1)} %copy-done.101) | copy-start | bytes 100
  90.2 37.1 %copy-start.12 = (bf16[256,1024]{0,1:T(8,128)(2,1)}, bf16[256,1024]{0,1:T(8,128)(2,1)S(1)}, u32[]{:S(2)}) copy-start(bf16[256,1024]{0,1:T(8,128)(2,1)S(1)} %copy.114) | copy-start | bytes 1572868
  121.7 23.5 %copy-start.34 = (f32[16,32,256]{2,1,0:T(8,128)}, f32[16,32,256]{2,1,0:T(8,128)S(1)}, u32[]{:S(2)}) copy-start(f32[16,32,256]{2,1,0:T(8,128)S(1)} %fusion.11) | copy-start | bytes 1572868
  127.4 17.8 %copy-start.144 = (f32[32]{0:T(128)}, f32[32]{0:T(128)S(1)}, u32[]{:S(2)}) copy-start(f32[32]{0:T(128)S(1)} %get-tuple-element.70) | copy-start | bytes 388
  127.4 72.6 %copy-start.93 = (bf16[32,1024]{1,0:T(8,128)(2,1)}, bf16[32,1024]{1,0:T(8,128)(2,1)S(1)}, u32[]{:S(2)}) copy-start(bf16[32,1024]{1,0:T(8,128)(2,1)S(1)} %get-tuple-element.122) | copy-start | bytes 196612
  127.4 83.4 %copy-start.23 = (f32[32,1024]{1,0:T(8,128)}, f32[32,1024]{1,0:T(8,128)S(1)}, u32[]{:S(2)}) copy-start(f32[32,1024]{1,0:T(8,128)S(1)} %get-tuple-element.71) | copy-start | bytes 393220
  127.4 17.8 %copy-start.121 = (f32[32]{0:T(128)}, f32[32]{0:T(128)S(1)}, u32[]{:S(2)}) copy-start(f32[32]{0:T(128)S(1)} %fusion.257) | copy-start | bytes 388
  127.5 17.7 %copy-start.57 = (bf16[32,1024]{1,0:T(8,128)(2,1)}, bf16[32,1024]{1,0:T(8,128)(2,1)S(1)}, u32[]{:S(2)}) copy-start(bf16[32,1024]{1,0:T(8,128)(2,1)S(1)} %multiply_convert_fusion.10) | copy-start | bytes 196612
  145.2 62.3 %copy-start.31 = (f32[32,4096]{1,0:T(8,128)}, f32[32,4096]{1,0:T(8,128)S(1)}, u32[]{:S(2)}) copy-start(f32[32,4096]{1,0:T(8,128)S(1)} %fusion.285) | copy-start | bytes 1572868
  213.0 11.1 copy-start.135
  218.9 130.5 %reduce-scatter.11.cloned.1.call-start = ((), (), s32[]{:S(2)}) async-start(), calls=%async_computation.14 | async-start | bytes 1179648 | tf_op jit(solution)/shard_map/reduce_scatter | solution.py:137
  241.6 395.0 %reduce-scatter.17.cloned.1.call-start = ((), (), s32[]{:S(2)}) async-start(), calls=%async_computation.17 | async-start | bytes 1179648 | tf_op jit(solution)/shard_map/reduce_scatter | solution.py:140
  532.4 26.8 %copy-start.20 = (f32[32,1024]{1,0:T(8,128)}, f32[32,1024]{1,0:T(8,128)S(1)}, u32[]{:S(2)}) copy-start(f32[32,1024]{1,0:T(8,128)S(1)} %get-tuple-element.79) | copy-start | bytes 393220
  532.4 26.8 %copy-start.120 = (f32[32]{0:T(128)}, f32[32]{0:T(128)S(1)}, u32[]{:S(2)}) copy-start(f32[32]{0:T(128)S(1)} %fusion.261) | copy-start | bytes 388
  533.4 12.8 slice-start
  569.6 133.3 %reduce-scatter.21.cloned.1.call-start = ((), (), s32[]{:S(2)}) async-start(), calls=%async_computation.19 | async-start | bytes 1179648 | tf_op jit(solution)/shard_map/reduce_scatter | solution.py:140
  578.9 190.0 %reduce-scatter.15.cloned.1.call-start = ((), (), s32[]{:S(2)}) async-start(), calls=%async_computation.16 | async-start | bytes 1179648 | tf_op jit(solution)/shard_map/reduce_scatter | solution.py:137
  581.9 253.1 %reduce-scatter.19.cloned.1.call-start = ((), (), s32[]{:S(2)}) async-start(), calls=%async_computation.18 | async-start | bytes 1179648 | tf_op jit(solution)/shard_map/reduce_scatter | solution.py:137
  586.8 363.5 %reduce-scatter.25.cloned.1.call-start = ((), (), s32[]{:S(2)}) async-start(), calls=%async_computation.21 | async-start | bytes 4325376 | tf_op jit(solution)/shard_map/reduce_scatter | solution.py:164
  590.7 245.2 %copy-start.62 = (bf16[32,1024]{1,0:T(8,128)(2,1)S(1)}, bf16[32,1024]{1,0:T(8,128)(2,1)}, u32[]{:S(2)}) copy-start(bf16[32,1024]{1,0:T(8,128)(2,1)} %copy-done.61) | copy-start | bytes 196612
  590.7 245.2 %copy-start.63 = (bf16[32,1024]{1,0:T(8,128)(2,1)S(1)}, bf16[32,1024]{1,0:T(8,128)(2,1)}, u32[]{:S(2)}) copy-start(bf16[32,1024]{1,0:T(8,128)(2,1)} %get-tuple-element.98) | copy-start | bytes 196612
  590.7 245.2 %copy-start.65 = (bf16[32,1024]{1,0:T(8,128)(2,1)S(1)}, bf16[32,1024]{1,0:T(8,128)(2,1)}, u32[]{:S(2)}) copy-start(bf16[32,1024]{1,0:T(8,128)(2,1)} %copy-done.64) | copy-start | bytes 196612
  590.7 245.2 %copy-start.66 = (bf16[32,1024]{1,0:T(8,128)(2,1)S(1)}, bf16[32,1024]{1,0:T(8,128)(2,1)}, u32[]{:S(2)}) copy-start(bf16[32,1024]{1,0:T(8,128)(2,1)} %reshape.451) | copy-start | bytes 196612
  590.7 245.2 %copy-start.67 = (bf16[32,1024]{1,0:T(8,128)(2,1)S(1)}, bf16[32,1024]{1,0:T(8,128)(2,1)}, u32[]{:S(2)}) copy-start(bf16[32,1024]{1,0:T(8,128)(2,1)} %convert.41) | copy-start | bytes 196612
  590.7 245.2 %copy-start.69 = (bf16[32,1024]{1,0:T(8,128)(2,1)S(1)}, bf16[32,1024]{1,0:T(8,128)(2,1)}, u32[]{:S(2)}) copy-start(bf16[32,1024]{1,0:T(8,128)(2,1)} %copy-done.68) | copy-start | bytes 196612
  590.8 544.8 %reduce-scatter.23.cloned.1.call-start = ((), (), s32[]{:S(2)}) async-start(), calls=%async_computation.20 | async-start | bytes 12976128 | tf_op jit(solution)/shard_map/reduce_scatter | solution.py:163
  591.3 251.0 %copy-start.72 = (bf16[32,1024]{1,0:T(8,128)(2,1)}, bf16[32,1024]{1,0:T(8,128)(2,1)S(1)}, u32[]{:S(2)}) copy-start(bf16[32,1024]{1,0:T(8,128)(2,1)S(1)} %reshape.459) | copy-start | bytes 196612
  591.8 250.5 %copy-start.70 = (bf16[32,1024]{1,0:T(8,128)(2,1)}, bf16[32,1024]{1,0:T(8,128)(2,1)S(1)}, u32[]{:S(2)}) copy-start(bf16[32,1024]{1,0:T(8,128)(2,1)S(1)} %reshape.455) | copy-start | bytes 196612
  637.5 204.8 %copy-start.74 = (bf16[32,1024]{1,0:T(8,128)(2,1)}, bf16[32,1024]{1,0:T(8,128)(2,1)S(1)}, u32[]{:S(2)}) copy-start(bf16[32,1024]{1,0:T(8,128)(2,1)S(1)} %convert.44) | copy-start | bytes 196612
  703.8 138.5 %copy-start.78 = (bf16[32,1024]{1,0:T(8,128)(2,1)}, bf16[32,1024]{1,0:T(8,128)(2,1)S(1)}, u32[]{:S(2)}) copy-start(bf16[32,1024]{1,0:T(8,128)(2,1)S(1)} %convert.47) | copy-start | bytes 196612
  769.8 72.5 %copy-start.76 = (bf16[32,1024]{1,0:T(8,128)(2,1)}, bf16[32,1024]{1,0:T(8,128)(2,1)S(1)}, u32[]{:S(2)}) copy-start(bf16[32,1024]{1,0:T(8,128)(2,1)S(1)} %convert.43) | copy-start | bytes 196612
  842.4 480.5 %reduce-scatter.29.cloned.1.call-start = ((), (), s32[]{:S(2)}) async-start(), calls=%async_computation.23 | async-start | bytes 17301504 | tf_op jit(solution)/shard_map/reduce_scatter | solution.py:167
  853.9 656.4 %reduce-scatter.27.cloned.1.call-start = ((), (), s32[]{:S(2)}) async-start(), calls=%async_computation.22 | async-start | bytes 17301504 | tf_op jit(solution)/shard_map/reduce_scatter | solution.py:166
  885.4 11.2 slice-start.4
  896.8 50.4 %copy-start.25 = (f32[32,1024]{1,0:T(8,128)S(1)}, f32[32,1024]{1,0:T(8,128)}, u32[]{:S(2)}) copy-start(f32[32,1024]{1,0:T(8,128)} %get-tuple-element.75) | copy-start | bytes 393220
  (118 other events, 508.2 us)
Sparse Core Ops, SparseCore 0:
  9.6 46.5 all-gather.5
  57.8 22.5 all-gather.7
  81.9 58.2 all-gather.9
  141.7 58.2 all-gather.11
  219.0 64.2 reduce-scatter.12
  287.0 62.4 reduce-scatter.10
  569.7 66.7 reduce-scatter.16
  640.4 62.4 reduce-scatter.20
  706.3 62.5 reduce-scatter.14
  772.5 62.4 reduce-scatter.18
  837.8 107.5 reduce-scatter.24
  951.9 183.5 reduce-scatter.22
  1138.5 184.4 reduce-scatter.28
  1325.8 184.4 reduce-scatter.26
where the time goes:
time: 1520 us
  waiting for transfers between devices  973 us (64%)
  blocking collectives  256 us (17%)
  matrix products  154 us (10%)
  local copies, waits for them, and re-layouts  63.5 us (4%)
  other arithmetic  53.5 us (4%)
  between operations  16.2 us (1%)
    reduce_scatter x3, waiting for transfers between devices, shards(): lax.psum_scatter(d_key_part.reshape(total, width), 'ctx', scatter_dimensi...  195 us
    reduce_scatter x1, waiting for transfers between devices, shards(): lax.psum_scatter(grad_down, ('ctx', 'fsdp'), scatter_dimension=0, tiled=T...  187 us
    reduce_scatter x1, waiting for transfers between devices, shards(): lax.psum_scatter(grad_up, ('ctx', 'fsdp'), scatter_dimension=0, tiled=True)  187 us
    reduce_scatter x1, waiting for transfers between devices, shards(): lax.psum_scatter(grad_qkv, ('ctx', 'fsdp'), scatter_dimension=0, tiled=True)  185 us
    reduce_scatter x3, waiting for transfers between devices, shards(): lax.psum_scatter(d_value_part.reshape(total, width), 'ctx', scatter_dimen...  138 us
    all_gather x3, blocking collectives, shards(): lax.all_gather(values_local, 'ctx', axis=0, tiled=True)  98.5 us
    all_gather x3, blocking collectives, shards(): lax.all_gather(keys_local, 'ctx', axis=0, tiled=True)  92.5 us
    all_gather x1, waiting for transfers between devices, fetch(): lax.all_gather(w_down, 'fsdp', axis=0, tiled=True)  54.8 us
  transfers between devices with their start and end apart: 14, of which 12 were waited for; matrix products, arithmetic and copies ran while one was open for 10% of the time, Pallas kernels for 0%

commit v1 on v0

--- a/solution.py
+++ b/solution.py
@@ -2,6 +2,7 @@
 import jax.numpy as jnp
 from jax import lax
 from jax.sharding import PartitionSpec as P
+from jax.lax import axis_index, ppermute, psum
 
 HEADS = 16
 HEAD_DIM = 64
@@ -9,6 +10,12 @@
 EPSILON = 1e-06
 MASKED = -1e30
 HIGHEST = lax.Precision.HIGHEST
+
+
+def finish_arrays(obj, along_dim):
+    t1 = list(obj.shape[1:])
+    t1[along_dim] *= obj.shape[0]
+    return jnp.moveaxis(obj, 0, along_dim).reshape(t1)
 
 
 def rms_norm(values, gain):
@@ -74,8 +81,28 @@
         queries = qkv[:, :width]
         keys_local = qkv[:, width : 2 * width]
         values_local = qkv[:, 2 * width :]
+
+        def finish_orders(lane_axis, d_out, x0):
+            devs = psum(1, lane_axis)
+            entries = tuple(((to_i, (to_i + 1) % devs) for to_i in range(devs)))
+            far_arr, top = ([], [])
+            heap = tuple(((hop_no, jj) for jj, hop_no in entries))
+            for j0 in tuple(range(devs - 1)):
+                if j0 % 2 == 0:
+                    shaped = ppermute(far_arr[-1] if far_arr else x0, lane_axis, entries)
+                    far_arr.append(shaped)
+                else:
+                    aux = ppermute(top[-1] if top else x0, lane_axis, heap)
+                    top.append(aux)
+            block_last = jnp.stack([*far_arr[::-1], x0, *top], axis=0)
+            outcome_arr = axis_index(lane_axis)
+            u1 = len(far_arr)
+            spare = outcome_arr - u1
+            block_last = block_last[(jnp.arange(devs) - spare) % devs]
+            return finish_arrays(block_last, d_out)
+
         keys_all, values_all = (
-            lax.all_gather(keys_local, "ctx", axis=0, tiled=True),
+            finish_orders("ctx", 0, keys_local),
             lax.all_gather(values_local, "ctx", axis=0, tiled=True),
         )
         total = keys_all.shape[0]

time: 1520 us -> 1510 us (level)
  blocking collectives: 256 us -> 167 us
  local copies, waits for them, and re-layouts: 63.5 us -> 102 us
  starting transfers between devices: 1.18 us -> 29.7 us
    all_gather x3 -> x0, blocking collectives: 92.5 us -> none  [shards(): lax.all_gather(keys_local, 'ctx', axis=0, tiled=True)]
    ppermute x0 -> x21, starting transfers between devices: none -> 28.8 us  [the longest x12 17.2 us: finish_orders(): shaped = ppermute(far_arr[-1] if far_arr else x0, lane_axis, entries)]
    unnamed x308 -> x321, local copies, waits for them, and re-layouts: 14.5 us -> 35.9 us
  transfers between devices with their start and end apart: 14 -> 35, of which waited for: 12 -> 17; matrix products, arithmetic and copies ran while one was open for 10% -> 14% of each run, Pallas kernels for 0% -> 0%
where the time goes in v1:
time: 1510 us
  waiting for transfers between devices  976 us (65%)
  blocking collectives  167 us (11%)
  matrix products  156 us (10%)
  local copies, waits for them, and re-layouts  102 us (7%)
  other arithmetic  61.7 us (4%)
  starting transfers between devices  29.7 us (2%)
  between operations  16.1 us (1%)
    reduce_scatter x3, waiting for transfers between devices, shards(): lax.psum_scatter(d_key_part.reshape(total, width), 'ctx', scatter_dimensi...  195 us
    reduce_scatter x1, waiting for transfers between devices, shards(): lax.psum_scatter(grad_down, ('ctx', 'fsdp'), scatter_dimension=0, tiled=T...  187 us
    reduce_scatter x1, waiting for transfers between devices, shards(): lax.psum_scatter(grad_up, ('ctx', 'fsdp'), scatter_dimension=0, tiled=True)  187 us
    reduce_scatter x1, waiting for transfers between devices, shards(): lax.psum_scatter(grad_qkv, ('ctx', 'fsdp'), scatter_dimension=0, tiled=True)  178 us
    reduce_scatter x3, waiting for transfers between devices, shards(): lax.psum_scatter(d_value_part.reshape(total, width), 'ctx', scatter_dimen...  140 us
    all_gather x3, blocking collectives, shards(): lax.all_gather(values_local, 'ctx', axis=0, tiled=True)  102 us
    all_gather x1, waiting for transfers between devices, fetch(): lax.all_gather(w_down, 'fsdp', axis=0, tiled=True)  54.8 us
    unnamed x1, blocking collectives  39.9 us
  transfers between devices with their start and end apart: 35, of which 17 were waited for; matrix products, arithmetic and copies ran while one was open for 14% of the time, Pallas kernels for 0%

profile of v1, /device:TPU:14, one launch (start us, length us, event | category | flops | bytes accessed | tf_op | source)
XLA Modules:
  0.0 1508.0 jit_solution(3940499111331921191)
XLA Ops:
  10.2 25.0 %all-gather = s32[8,32,3]{1,2,0:T(4,128)S(1)} all-gather(s32[1,32,3]{1,2,0:T(4,128)S(1)} %bitcast.330), channel_id=1, replica_groups=mesh['ctx'=8,'fsdp'=4] {'ctx'}, dimensions={0}, use_global_device_ids=true | all-gather | bytes 3456 | tf_op jit(solution)/shard_map/all_gather | solution.py:64
  43.3 12.9 all-gather.6.cloned.1.call-done
  56.2 4.0 convolution_convert_fusion.2
  69.7 3.3 collective-permute-start.2
  74.9 3.3 collective-permute-start.3
  78.2 33.4 %all_gather.33 = bf16[256,1024]{1,0:T(8,128)(2,1)S(1)} all-gather(bf16[32,1024]{1,0:T(8,128)(2,1)} %get-tuple-element.90), channel_id=1, replica_groups=mesh['ctx'=8,'fsdp'=4] {'ctx'}, dimensions={0}, use_global_device_ids=true | all-gather | bytes 589824 | tf_op jit(solution)/shard_map/all_gather | solution.py:106
  127.6 12.7 all-gather.10.cloned.1.call-done
  140.3 4.9 fusion.287
  145.3 54.8 %all-gather.12.cloned.1.call-done = bf16[4096,1024]{1,0:T(8,128)(2,1)} async-done(((bf16[1024,1024]{1,0:T(8,128)(2,1)}), bf16[4096,1024]{1,0:T(8,128)(2,1)}) %all-gather.12.cloned.1.call-update) | async-done | bytes 8388624 | tf_op jit(solution)/shard_map/all_gather | solution.py:35
  200.0 7.5 add_convert_fusion.2
  207.6 3.2 multiply_reduce_fusion.5
  213.0 3.4 fusion.164
  248.4 5.6 convolution_add_fusion.2
  254.0 29.4 %reduce-scatter.13.cloned.1.call-done = f32[32,1024]{1,0:T(8,128)} async-done(((f32[256,1024]{1,0:T(8,128)}), f32[32,1024]{1,0:T(8,128)}) %reduce-scatter.13.cloned.1.call-update) | async-done | bytes 131088 | tf_op jit(solution)/shard_map/reduce_scatter | solution.py:167
  284.9 64.6 %reduce-scatter.11.cloned.1.call-done = f32[32,1024]{1,0:T(8,128)} async-done(((f32[256,1024]{1,0:T(8,128)}), f32[32,1024]{1,0:T(8,128)}) %reduce-scatter.11.cloned.1.call-update) | async-done | bytes 131088 | tf_op jit(solution)/shard_map/reduce_scatter | solution.py:164
  350.4 6.3 multiply_reduce_fusion.8
  356.7 4.0 convolution_convert_fusion.1
  362.0 4.0 convolution_convert_fusion
  375.8 33.0 %all_gather.38 = bf16[256,1024]{1,0:T(8,128)(2,1)} all-gather(bf16[32,1024]{1,0:T(8,128)(2,1)S(1)} %get-tuple-element.93), channel_id=1, replica_groups=mesh['ctx'=8,'fsdp'=4] {'ctx'}, dimensions={0}, use_global_device_ids=true | all-gather | bytes 589824 | tf_op jit(solution)/shard_map/all_gather | solution.py:106
  409.0 4.3 collective-permute-start.12
  413.9 35.3 %all_gather.39 = bf16[256,1024]{1,0:T(8,128)(2,1)} all-gather(bf16[32,1024]{1,0:T(8,128)(2,1)S(1)} %get-tuple-element.96), channel_id=1, replica_groups=mesh['ctx'=8,'fsdp'=4] {'ctx'}, dimensions={0}, use_global_device_ids=true | all-gather | bytes 589824 | tf_op jit(solution)/shard_map/all_gather | solution.py:106
  456.7 4.3 collective-permute-start.13
  514.8 3.0 fusion.17
  524.2 5.1 fusion.288
  529.4 7.6 add_convert_fusion.1
  537.1 3.2 multiply_reduce_fusion.4
  542.5 4.5 add_convert_fusion
  547.0 3.2 multiply_reduce_fusion.3
  554.7 3.3 fusion.158
  563.9 3.3 fusion.152
  577.8 3.8 fusion.104
  582.7 44.9 %reduce-scatter.17.cloned.1.call-done = f32[32,1024]{1,0:T(8,128)} async-done(((f32[256,1024]{1,0:T(8,128)}), f32[32,1024]{1,0:T(8,128)}) %reduce-scatter.17.cloned.1.call-update) | async-done | bytes 131088 | tf_op jit(solution)/shard_map/reduce_scatter | solution.py:167
  628.6 65.3 %reduce-scatter.21.cloned.1.call-done = f32[32,1024]{1,0:T(8,128)} async-done(((f32[256,1024]{1,0:T(8,128)}), f32[32,1024]{1,0:T(8,128)}) %reduce-scatter.21.cloned.1.call-update) | async-done | bytes 131088 | tf_op jit(solution)/shard_map/reduce_scatter | solution.py:167
  694.8 65.0 %reduce-scatter.15.cloned.1.call-done = f32[32,1024]{1,0:T(8,128)} async-done(((f32[256,1024]{1,0:T(8,128)}), f32[32,1024]{1,0:T(8,128)}) %reduce-scatter.15.cloned.1.call-update) | async-done | bytes 131088 | tf_op jit(solution)/shard_map/reduce_scatter | solution.py:164
  760.6 65.2 %reduce-scatter.19.cloned.1.call-done = f32[32,1024]{1,0:T(8,128)} async-done(((f32[256,1024]{1,0:T(8,128)}), f32[32,1024]{1,0:T(8,128)}) %reduce-scatter.19.cloned.1.call-update) | async-done | bytes 131088 | tf_op jit(solution)/shard_map/reduce_scatter | solution.py:164
  826.9 6.4 fusion.45
  836.8 8.2 fusion.39
  846.1 8.1 fusion.33
  863.6 5.1 convolution_add_fusion.1
  870.1 6.0 convolution_add_fusion
  876.1 3.5 scatter_custom_fusion.2
  886.0 4.9 fusion.93
  891.1 3.3 multiply_reduce_fusion.7
  894.4 3.6 scatter_custom_fusion.5
  901.3 39.9 %all-reduce.3 = (f32[1024]{0:T(1024)S(1)}, f32[1024]{0:T(1024)S(1)}, f32[1024]{0:T(1024)S(1)}) all-reduce(f32[1024]{0:T(1024)S(1)} %add_add_fusion.11, f32[1024]{0:T(1024)S(1)} %add_add_fusion.10, f32[1024]{0:T(1024)} %add_add_fusion.9), channel_id=8, replica_groups=mesh['ctx'=8,'fsdp'=4] {'ctx','fsdp'}, use_global_device_ids=true, to_apply=%region_37.39.clone | all-reduce | flops 3072 | bytes 24576
  948.1 178.4 %reduce-scatter.23.cloned.1.call-done = f32[32,3072]{1,0:T(8,128)} async-done(((f32[1024,3072]{1,0:T(8,128)}), f32[32,3072]{1,0:T(8,128)}) %reduce-scatter.23.cloned.1.call-update) | async-done | bytes 393232 | tf_op jit(solution)/shard_map/reduce_scatter | solution.py:190
  1126.5 187.4 %reduce-scatter.29.cloned.1.call-done = f32[128,1024]{1,0:T(8,128)} async-done(((f32[4096,1024]{1,0:T(8,128)}), f32[128,1024]{1,0:T(8,128)}) %reduce-scatter.29.cloned.1.call-update) | async-done | bytes 524304 | tf_op jit(solution)/shard_map/reduce_scatter | solution.py:194
  1313.9 187.3 %reduce-scatter.27.cloned.1.call-done = f32[32,4096]{1,0:T(8,128)} async-done(((f32[1024,4096]{1,0:T(8,128)}), f32[32,4096]{1,0:T(8,128)}) %reduce-scatter.27.cloned.1.call-update) | async-done | bytes 524304 | tf_op jit(solution)/shard_map/reduce_scatter | solution.py:193
  (537 shorter events, 213.3 us)
Async XLA Ops:
  7.2 49.0 %all-gather.6.cloned.1.call-start = ((), (), s32[]{:S(2)}) async-start(), calls=%async_computation.10 | async-start | bytes 7864320 | tf_op jit(solution)/shard_map/all_gather | solution.py:32
  7.9 116.7 %all-gather.8.cloned.1.call-start = ((), (), s32[]{:S(2)}) async-start(), calls=%async_computation.11 | async-start | bytes 2621440 | tf_op jit(solution)/shard_map/all_gather | solution.py:33
  8.7 131.6 %all-gather.10.cloned.1.call-start = ((), (), s32[]{:S(2)}) async-start(), calls=%async_computation.12 | async-start | bytes 10485760 | tf_op jit(solution)/shard_map/all_gather | solution.py:34
  9.4 190.6 %all-gather.12.cloned.1.call-start = ((), (), s32[]{:S(2)}) async-start(), calls=%async_computation.13 | async-start | bytes 10485760 | tf_op jit(solution)/shard_map/all_gather | solution.py:35
  10.0 273.3 %reduce-scatter.13.cloned.1.call-start = ((), (), s32[]{:S(2)}) async-start(), calls=%async_computation.15 | async-start | bytes 1179648 | tf_op jit(solution)/shard_map/reduce_scatter | solution.py:167
  60.9 4.5 collective-permute-start
  63.7 147.1 %copy-start.21 = (f32[32,1024]{1,0:T(8,128)}, f32[32,1024]{1,0:T(8,128)S(1)}, u32[]{:S(2)}) copy-start(f32[32,1024]{1,0:T(8,128)S(1)} %gather_fusion.6) | copy-start | bytes 393220
  65.4 4.3 collective-permute-start.1
  67.8 5.4 collective-permute-start.4
  69.7 5.2 collective-permute-start.2
  73.2 39.6 %collective-permute-start.5 = (bf16[32,1024]{1,0:T(8,128)(2,1)S(1)}, bf16[32,1024]{1,0:T(8,128)(2,1)}, u32[]{:S(2)}, u32[]{:S(2)}) collective-permute-start(bf16[32,1024]{1,0:T(8,128)(2,1)S(1)} %collective-permute-done.4), channel_id=1, source_target_pairs={{4,0},{8,4},{12,8},{16,12},{20,16},{24,20},{28,24},{0,28},{5,1},{9... | collective-permute-start | bytes 196616 | tf_op jit(solution)/shard_map/ppermute | solution.py:95
  74.9 38.5 %collective-permute-start.3 = (bf16[32,1024]{1,0:T(8,128)(2,1)S(1)}, bf16[32,1024]{1,0:T(8,128)(2,1)}, u32[]{:S(2)}, u32[]{:S(2)}) collective-permute-start(bf16[32,1024]{1,0:T(8,128)(2,1)S(1)} %collective-permute-done.2), channel_id=1, source_target_pairs={{0,4},{4,8},{8,12},{12,16},{16,20},{20,24},{24,28},{28,0},{1,5},{5... | collective-permute-start | bytes 196616 | tf_op jit(solution)/shard_map/ppermute | solution.py:92
  112.8 6.5 collective-permute-start.6
  127.5 83.4 %copy-start.22 = (f32[32,1024]{1,0:T(8,128)}, f32[32,1024]{1,0:T(8,128)S(1)}, u32[]{:S(2)}) copy-start(f32[32,1024]{1,0:T(8,128)S(1)} %get-tuple-element.71) | copy-start | bytes 393220
  218.9 130.6 %reduce-scatter.11.cloned.1.call-start = ((), (), s32[]{:S(2)}) async-start(), calls=%async_computation.14 | async-start | bytes 1179648 | tf_op jit(solution)/shard_map/reduce_scatter | solution.py:164
  240.4 387.2 %reduce-scatter.17.cloned.1.call-start = ((), (), s32[]{:S(2)}) async-start(), calls=%async_computation.17 | async-start | bytes 1179648 | tf_op jit(solution)/shard_map/reduce_scatter | solution.py:167
  361.4 7.4 collective-permute-start.7
  367.4 5.6 collective-permute-start.14
  368.8 80.4 %copy-start.99 = (bf16[32,1024]{1,0:T(8,128)(2,1)}, bf16[32,1024]{1,0:T(8,128)(2,1)S(1)}, u32[]{:S(2)}) copy-start(bf16[32,1024]{1,0:T(8,128)(2,1)S(1)} %collective-permute-done.7) | copy-start | bytes 196612
  368.8 5.7 collective-permute-start.8
  370.8 38.0 %collective-permute-start.18 = (bf16[32,1024]{1,0:T(8,128)(2,1)S(1)}, bf16[32,1024]{1,0:T(8,128)(2,1)}, u32[]{:S(2)}, u32[]{:S(2)}) collective-permute-start(bf16[32,1024]{1,0:T(8,128)(2,1)S(1)} %get-tuple-element.95), channel_id=1, source_target_pairs={{4,0},{8,4},{12,8},{16,12},{20,16},{24,20},{28,24},{0,28},{5,1},{9... | collective-permute-start | bytes 196616 | tf_op jit(solution)/shard_map/ppermute | solution.py:95
  371.5 37.4 %collective-permute-start.11 = (bf16[32,1024]{1,0:T(8,128)(2,1)S(1)}, bf16[32,1024]{1,0:T(8,128)(2,1)}, u32[]{:S(2)}, u32[]{:S(2)}) collective-permute-start(bf16[32,1024]{1,0:T(8,128)(2,1)S(1)} %get-tuple-element.92), channel_id=1, source_target_pairs={{4,0},{8,4},{12,8},{16,12},{20,16},{24,20},{28,24},{0,28},{5,1},{9... | collective-permute-start | bytes 196616 | tf_op jit(solution)/shard_map/ppermute | solution.py:95
  373.0 40.3 %collective-permute-start.15 = (bf16[32,1024]{1,0:T(8,128)(2,1)S(1)}, bf16[32,1024]{1,0:T(8,128)(2,1)}, u32[]{:S(2)}, u32[]{:S(2)}) collective-permute-start(bf16[32,1024]{1,0:T(8,128)(2,1)S(1)} %collective-permute-done.14), channel_id=1, source_target_pairs={{0,4},{4,8},{8,12},{12,16},{16,20},{20,24},{24,28},{28,0},{1,5},{5... | collective-permute-start | bytes 196616 | tf_op jit(solution)/shard_map/ppermute | solution.py:92
  374.5 38.8 %collective-permute-start.9 = (bf16[32,1024]{1,0:T(8,128)(2,1)S(1)}, bf16[32,1024]{1,0:T(8,128)(2,1)}, u32[]{:S(2)}, u32[]{:S(2)}) collective-permute-start(bf16[32,1024]{1,0:T(8,128)(2,1)S(1)} %collective-permute-done.8), channel_id=1, source_target_pairs={{0,4},{4,8},{8,12},{12,16},{16,20},{20,24},{24,28},{28,0},{1,5},{5... | collective-permute-start | bytes 196616 | tf_op jit(solution)/shard_map/ppermute | solution.py:92
  408.8 47.9 %collective-permute-start.19 = (bf16[32,1024]{1,0:T(8,128)(2,1)}, bf16[32,1024]{1,0:T(8,128)(2,1)}, u32[]{:S(2)}, u32[]{:S(2)}) collective-permute-start(bf16[32,1024]{1,0:T(8,128)(2,1)} %collective-permute-done.18), channel_id=1, source_target_pairs={{4,0},{8,4},{12,8},{16,12},{20,16},{24,20},{28,24},{0,28},{5,1},{9... | collective-permute-start | bytes 196616 | tf_op jit(solution)/shard_map/ppermute | solution.py:95
  409.0 47.7 %collective-permute-start.12 = (bf16[32,1024]{1,0:T(8,128)(2,1)}, bf16[32,1024]{1,0:T(8,128)(2,1)}, u32[]{:S(2)}, u32[]{:S(2)}) collective-permute-start(bf16[32,1024]{1,0:T(8,128)(2,1)} %collective-permute-done.11), channel_id=1, source_target_pairs={{4,0},{8,4},{12,8},{16,12},{20,16},{24,20},{28,24},{0,28},{5,1},{9... | collective-permute-start | bytes 196616 | tf_op jit(solution)/shard_map/ppermute | solution.py:95
  413.3 47.7 %collective-permute-start.16 = (bf16[32,1024]{1,0:T(8,128)(2,1)}, bf16[32,1024]{1,0:T(8,128)(2,1)}, u32[]{:S(2)}, u32[]{:S(2)}) collective-permute-start(bf16[32,1024]{1,0:T(8,128)(2,1)} %collective-permute-done.15), channel_id=1, source_target_pairs={{0,4},{4,8},{8,12},{12,16},{16,20},{20,24},{24,28},{28,0},{1,5},{5... | collective-permute-start | bytes 196616 | tf_op jit(solution)/shard_map/ppermute | solution.py:92
  413.3 47.7 %collective-permute-start.10 = (bf16[32,1024]{1,0:T(8,128)(2,1)}, bf16[32,1024]{1,0:T(8,128)(2,1)}, u32[]{:S(2)}, u32[]{:S(2)}) collective-permute-start(bf16[32,1024]{1,0:T(8,128)(2,1)} %collective-permute-done.9), channel_id=1, source_target_pairs={{0,4},{4,8},{8,12},{12,16},{16,20},{20,24},{24,28},{28,0},{1,5},{5... | collective-permute-start | bytes 196616 | tf_op jit(solution)/shard_map/ppermute | solution.py:92
  456.6 27.2 %collective-permute-start.20 = (bf16[32,1024]{1,0:T(8,128)(2,1)}, bf16[32,1024]{1,0:T(8,128)(2,1)}, u32[]{:S(2)}, u32[]{:S(2)}) collective-permute-start(bf16[32,1024]{1,0:T(8,128)(2,1)} %collective-permute-done.19), channel_id=1, source_target_pairs={{4,0},{8,4},{12,8},{16,12},{20,16},{24,20},{28,24},{0,28},{5,1},{9... | collective-permute-start | bytes 196616 | tf_op jit(solution)/shard_map/ppermute | solution.py:95
  456.7 24.1 %collective-permute-start.13 = (bf16[32,1024]{1,0:T(8,128)(2,1)}, bf16[32,1024]{1,0:T(8,128)(2,1)S(1)}, u32[]{:S(2)}, u32[]{:S(2)}) collective-permute-start(bf16[32,1024]{1,0:T(8,128)(2,1)} %collective-permute-done.12), channel_id=1, source_target_pairs={{4,0},{8,4},{12,8},{16,12},{20,16},{24,20},{28,24},{0,28},{5,1},{9... | collective-permute-start | bytes 196616 | tf_op jit(solution)/shard_map/ppermute | solution.py:95
  461.0 7.3 collective-permute-start.17
  560.6 133.3 %reduce-scatter.21.cloned.1.call-start = ((), (), s32[]{:S(2)}) async-start(), calls=%async_computation.19 | async-start | bytes 1179648 | tf_op jit(solution)/shard_map/reduce_scatter | solution.py:167
  569.8 189.9 %reduce-scatter.15.cloned.1.call-start = ((), (), s32[]{:S(2)}) async-start(), calls=%async_computation.16 | async-start | bytes 1179648 | tf_op jit(solution)/shard_map/reduce_scatter | solution.py:164
  572.8 253.0 %reduce-scatter.19.cloned.1.call-start = ((), (), s32[]{:S(2)}) async-start(), calls=%async_computation.18 | async-start | bytes 1179648 | tf_op jit(solution)/shard_map/reduce_scatter | solution.py:164
  577.8 370.3 %reduce-scatter.25.cloned.1.call-start = ((), (), s32[]{:S(2)}) async-start(), calls=%async_computation.21 | async-start | bytes 4325376 | tf_op jit(solution)/shard_map/reduce_scatter | solution.py:191
  581.6 245.2 %copy-start.63 = (bf16[32,1024]{1,0:T(8,128)(2,1)S(1)}, bf16[32,1024]{1,0:T(8,128)(2,1)}, u32[]{:S(2)}) copy-start(bf16[32,1024]{1,0:T(8,128)(2,1)} %copy-done.62) | copy-start | bytes 196612
  581.6 245.2 %copy-start.65 = (bf16[32,1024]{1,0:T(8,128)(2,1)S(1)}, bf16[32,1024]{1,0:T(8,128)(2,1)}, u32[]{:S(2)}) copy-start(bf16[32,1024]{1,0:T(8,128)(2,1)} %copy-done.64) | copy-start | bytes 196612
  581.6 245.2 %copy-start.67 = (bf16[32,1024]{1,0:T(8,128)(2,1)S(1)}, bf16[32,1024]{1,0:T(8,128)(2,1)}, u32[]{:S(2)}) copy-start(bf16[32,1024]{1,0:T(8,128)(2,1)} %copy-done.66) | copy-start | bytes 196612
  581.6 245.2 %copy-start.68 = (bf16[32,1024]{1,0:T(8,128)(2,1)S(1)}, bf16[32,1024]{1,0:T(8,128)(2,1)}, u32[]{:S(2)}) copy-start(bf16[32,1024]{1,0:T(8,128)(2,1)} %reshape.488) | copy-start | bytes 196612
  581.6 245.2 %copy-start.69 = (bf16[32,1024]{1,0:T(8,128)(2,1)S(1)}, bf16[32,1024]{1,0:T(8,128)(2,1)}, u32[]{:S(2)}) copy-start(bf16[32,1024]{1,0:T(8,128)(2,1)} %convert.41) | copy-start | bytes 196612
  581.6 245.2 %copy-start.71 = (bf16[32,1024]{1,0:T(8,128)(2,1)S(1)}, bf16[32,1024]{1,0:T(8,128)(2,1)}, u32[]{:S(2)}) copy-start(bf16[32,1024]{1,0:T(8,128)(2,1)} %copy-done.70) | copy-start | bytes 196612
  581.7 544.8 %reduce-scatter.23.cloned.1.call-start = ((), (), s32[]{:S(2)}) async-start(), calls=%async_computation.20 | async-start | bytes 12976128 | tf_op jit(solution)/shard_map/reduce_scatter | solution.py:190
  582.2 251.1 %copy-start.74 = (bf16[32,1024]{1,0:T(8,128)(2,1)}, bf16[32,1024]{1,0:T(8,128)(2,1)S(1)}, u32[]{:S(2)}) copy-start(bf16[32,1024]{1,0:T(8,128)(2,1)S(1)} %reshape.496) | copy-start | bytes 196612
  582.7 250.6 %copy-start.72 = (bf16[32,1024]{1,0:T(8,128)(2,1)}, bf16[32,1024]{1,0:T(8,128)(2,1)S(1)}, u32[]{:S(2)}) copy-start(bf16[32,1024]{1,0:T(8,128)(2,1)S(1)} %reshape.492) | copy-start | bytes 196612
  628.6 204.7 %copy-start.75 = (bf16[32,1024]{1,0:T(8,128)(2,1)}, bf16[32,1024]{1,0:T(8,128)(2,1)S(1)}, u32[]{:S(2)}) copy-start(bf16[32,1024]{1,0:T(8,128)(2,1)S(1)} %convert.44) | copy-start | bytes 196612
  694.8 138.5 %copy-start.79 = (bf16[32,1024]{1,0:T(8,128)(2,1)}, bf16[32,1024]{1,0:T(8,128)(2,1)S(1)}, u32[]{:S(2)}) copy-start(bf16[32,1024]{1,0:T(8,128)(2,1)S(1)} %convert.47) | copy-start | bytes 196612
  833.4 480.5 %reduce-scatter.29.cloned.1.call-start = ((), (), s32[]{:S(2)}) async-start(), calls=%async_computation.23 | async-start | bytes 17301504 | tf_op jit(solution)/shard_map/reduce_scatter | solution.py:194
  845.0 656.2 %reduce-scatter.27.cloned.1.call-start = ((), (), s32[]{:S(2)}) async-start(), calls=%async_computation.22 | async-start | bytes 17301504 | tf_op jit(solution)/shard_map/reduce_scatter | solution.py:193
  (135 other events, 1574.9 us)
Sparse Core Ops, SparseCore 0:
  9.6 46.5 all-gather.5
  57.8 22.5 all-gather.7
  82.0 58.2 all-gather.9
  141.7 58.2 all-gather.11
  219.0 64.3 reduce-scatter.12
  287.0 62.4 reduce-scatter.10
  560.7 66.9 reduce-scatter.16
  631.4 62.3 reduce-scatter.20
  697.3 62.4 reduce-scatter.14
  763.4 62.4 reduce-scatter.18
  828.7 107.7 reduce-scatter.24
  943.0 183.5 reduce-scatter.22
  1129.5 184.4 reduce-scatter.28
  1316.8 184.4 reduce-scatter.26
